TPU v7x, 32 devices: a whole 2x2x4 slice. The times are simulated.
32 devices in a mesh: ctx: 8 (over y, x, core), wshard: 4 (over z).
Axes of the slice: x: 2, y: 2, z: 4, core: 2. Of those that a mesh axis runs over, the one named last changes fastest.
Arguments:
- byte_feats: bfloat16 [8, 2048, 768], P('wshard', 'ctx'), may hold values from -6 to 6
- lengths: int32 [8], P('wshard'), may hold values from 512 to 2048, as said below
- latent_array: bfloat16 [256, 1280], P('wshard'), may hold values from -6 to 6
- lat_gain: bfloat16 [1280], P('wshard'), may hold values from 0.5 to 1.5
- lat_bias: bfloat16 [1280], P('wshard'), may hold values from -4 to 4
- in_gain: bfloat16 [768], P('wshard'), may hold values from 0.5 to 1.5
- in_bias: bfloat16 [768], P('wshard'), may hold values from -4 to 4
- w_query: bfloat16 [1280, 256], P('wshard'), may hold values from -0.25 to 0.25
- w_key: bfloat16 [768, 256], P('wshard'), may hold values from -0.3125 to 0.3125
- w_value: bfloat16 [768, 1280], P('wshard'), may hold values from -0.21875 to 0.21875
- w_output: bfloat16 [1280, 1280], P('wshard'), may hold values from -2 to 2
- mlp_gain: bfloat16 [1280], P('wshard'), may hold values from 0.5 to 1.5
- mlp_bias: bfloat16 [1280], P('wshard'), may hold values from -4 to 4
- w_up: bfloat16 [1280, 1280], P('wshard'), may hold values from -0.15625 to 0.15625
- w_down: bfloat16 [1280, 1280], P('wshard'), may hold values from -0.15625 to 0.15625
- cotangent: bfloat16 [8, 256, 1280], P('wshard'), may hold values from -6 to 6
Outputs:
- latents_out: bfloat16 [8, 256, 1280], P('wshard')
- byte_grad: bfloat16 [8, 2048, 768], P('wshard', 'ctx')
- grad_latent: float32 [256, 1280], P('wshard')
- grad_lat_gain: float32 [1280], P('wshard')
- grad_lat_bias: float32 [1280], P('wshard')
- grad_in_gain: float32 [768], P('wshard')
- grad_in_bias: float32 [768], P('wshard')
- grad_query: float32 [1280, 256], P('wshard')
- grad_key: float32 [768, 256], P('wshard')
- grad_value: float32 [768, 1280], P('wshard')
- grad_output: float32 [1280, 1280], P('wshard')
- grad_mlp_gain: float32 [1280], P('wshard')
- grad_mlp_bias: float32 [1280], P('wshard')
- grad_up: float32 [1280, 1280], P('wshard')
- grad_down: float32 [1280, 1280], P('wshard')
Inputs may be any that keep to these rules, and one draw needn't show every extreme that they name: The first lengths[s] slots of sequence s hold bytes, the rest are padding; some sequence fills all 2048 slots.
All inputs are finite; a program needn't handle non-finite values.
Results may differ from a plain program's by a relative error of at most 0.019.
Values may be sent and summed in bfloat16 or wider, within the bound.
A program may use at most 256 MiB of HBM per device.

v0:
```python
import math
import jax
import jax.numpy as jnp
from jax import lax
from jax.sharding import PartitionSpec as P

H = 8


def layer_norm(values, gain, offset):
    center = jnp.mean(values, axis=-1, keepdims=True)
    centred = values - center
    variance = jnp.mean(centred * centred, axis=-1, keepdims=True)
    return centred * lax.rsqrt(variance + 1e-05) * gain + offset


def exact_gelu(values):
    return jax.nn.gelu(values, approximate=False)


def matmul(left, right):
    return jnp.dot(left, right, preferred_element_type=jnp.float32)


def combine(first, second):
    top_first, sum_first, num_first = first
    top_second, sum_second, num_second = second
    highest = jnp.maximum(top_first, top_second)
    weight_first = jnp.exp(top_first - highest)
    weight_second = jnp.exp(top_second - highest)
    return (
        highest,
        sum_first * weight_first + sum_second * weight_second,
        num_first * weight_first[..., None] + num_second * weight_second[..., None],
    )


def block_stats(queries, keys, values, start, length, score_scale):
    row_count = keys.shape[0]
    head_count = queries.shape[1]
    kheads = keys.reshape(row_count, head_count, -1)
    vheads = values.reshape(row_count, head_count, -1)
    scores = (
        jnp.einsum("lhd,khd->hlk", queries, kheads, preferred_element_type=jnp.float32)
        * score_scale
    )
    valid = start + lax.iota(jnp.int32, row_count) < length
    masked = jnp.where(valid, scores, -1e30)
    highest = jnp.max(masked, axis=-1)
    weights = jnp.where(valid, jnp.exp(masked - highest[..., None]), 0.0)
    numer = jnp.einsum(
        "hlk,khe->hle", weights.astype(jnp.bfloat16), vheads, preferred_element_type=jnp.float32
    )
    return (highest, jnp.sum(weights, axis=-1), numer)


def query_part(queries, grad_heads, log_total, delta, keys, values, start, length, score_scale):
    row_count = keys.shape[0]
    head_count = queries.shape[1]
    kheads = keys.reshape(row_count, head_count, -1)
    vheads = values.reshape(row_count, head_count, -1)
    scores = (
        jnp.einsum("lhd,khd->hlk", queries, kheads, preferred_element_type=jnp.float32)
        * score_scale
    )
    valid = start + lax.iota(jnp.int32, row_count) < length
    probs = jnp.where(valid, jnp.exp(scores - log_total[..., None]), 0.0)
    dprobs = jnp.einsum("lhe,khe->hlk", grad_heads, vheads, preferred_element_type=jnp.float32)
    dscores = (probs * (dprobs - delta[..., None])).astype(jnp.bfloat16)
    dquery = (
        jnp.einsum("hlk,khd->lhd", dscores, kheads, preferred_element_type=jnp.float32)
        * score_scale
    )
    return (dquery, dscores, probs)


def blocked(block_fn, carry, keys, values):
    row_count = keys.shape[0]
    block_size = math.gcd(row_count, 1024)
    block_count = row_count // block_size
    key_blocks = keys.reshape(block_count, block_size, keys.shape[1])
    value_blocks = values.reshape(block_count, block_size, values.shape[1])

    def scan_step(carried, block_item):
        key_block, value_block, offset = block_item
        return (block_fn(carried, key_block, value_block, offset * block_size), None)

    result, _ = lax.scan(
        scan_step, carry, (key_blocks, value_blocks, jnp.arange(block_count, dtype=jnp.int32))
    )
    return result


def shards(
    byte_feats,
    lengths,
    latent_array,
    lat_gain,
    lat_bias,
    in_gain,
    in_bias,
    w_query,
    w_key,
    w_value,
    w_output,
    mlp_gain,
    mlp_bias,
    w_up,
    w_down,
    cotangent,
):
    head_count = H
    micro_count = byte_feats.shape[0]
    slot_count = byte_feats.shape[1]
    key_start = lax.axis_index("ctx") * slot_count
    latent_outs = []
    byte_grads = []
    totals = None
    for micro_step in range(micro_count):
        gathered = (
            lax.all_gather(latent_array, "wshard", axis=0, tiled=True),
            lax.all_gather(lat_gain, "wshard", axis=0, tiled=True),
            lax.all_gather(lat_bias, "wshard", axis=0, tiled=True),
            lax.all_gather(in_gain, "wshard", axis=0, tiled=True),
            lax.all_gather(in_bias, "wshard", axis=0, tiled=True),
            lax.all_gather(w_query, "wshard", axis=0, tiled=True),
            lax.all_gather(w_key, "wshard", axis=0, tiled=True),
            lax.all_gather(w_value, "wshard", axis=0, tiled=True),
            lax.all_gather(w_output, "wshard", axis=0, tiled=True),
            lax.all_gather(mlp_gain, "wshard", axis=0, tiled=True),
            lax.all_gather(mlp_bias, "wshard", axis=0, tiled=True),
            lax.all_gather(w_up, "wshard", axis=0, tiled=True),
            lax.all_gather(w_down, "wshard", axis=0, tiled=True),
        )
        (
            latent,
            gain_lat,
            bias_lat,
            gain_in,
            bias_in,
            query_w,
            key_w,
            value_w,
            output_w,
            gain_mlp,
            bias_mlp,
            up_w,
            down_w,
        ) = gathered
        length = lengths[micro_step]
        features = byte_feats[micro_step].astype(jnp.float32)
        normed_in, in_back = jax.vjp(
            layer_norm, features, gain_in.astype(jnp.float32), bias_in.astype(jnp.float32)
        )
        input_low = normed_in.astype(jnp.bfloat16)
        keys = matmul(input_low, key_w).astype(jnp.bfloat16)
        values = matmul(input_low, value_w).astype(jnp.bfloat16)
        latent_full = latent.astype(jnp.float32)
        normed_lat, lat_back = jax.vjp(
            layer_norm, latent_full, gain_lat.astype(jnp.float32), bias_lat.astype(jnp.float32)
        )
        lat_low = normed_lat.astype(jnp.bfloat16)
        head_size = query_w.shape[1] // head_count
        score_scale = 1.0 / math.sqrt(head_size)
        queries = matmul(lat_low, query_w).astype(jnp.bfloat16).reshape(-1, head_count, head_size)
        lat_rows = queries.shape[0]
        value_head = values.shape[1] // head_count
        empty = (
            jnp.full((head_count, lat_rows), -1e30, jnp.float32),
            jnp.zeros((head_count, lat_rows), jnp.float32),
            jnp.zeros((head_count, lat_rows, value_head), jnp.float32),
        )

        def add_block(carried, key_block, value_block, block_start):
            return combine(
                carried,
                block_stats(queries, key_block, value_block, block_start, length, score_scale),
            )

        highest, total, numer = blocked(
            add_block,
            empty,
            lax.all_gather(keys, "ctx", axis=0, tiled=True),
            lax.all_gather(values, "ctx", axis=0, tiled=True),
        )
        attended = numer / total[..., None]
        log_total = highest + jnp.log(total)
        att_low = jnp.transpose(attended, (1, 0, 2)).reshape(lat_rows, -1).astype(jnp.bfloat16)
        hidden = latent_full + matmul(att_low, output_w)
        normed_mid, mid_back = jax.vjp(
            layer_norm, hidden, gain_mlp.astype(jnp.float32), bias_mlp.astype(jnp.float32)
        )
        mid_low = normed_mid.astype(jnp.bfloat16)
        upward = matmul(mid_low, up_w)
        activated, gelu_back = jax.vjp(exact_gelu, upward)
        act_low = activated.astype(jnp.bfloat16)
        result = hidden + matmul(act_low, down_w)
        latent_outs.append(result.astype(jnp.bfloat16))
        dout = cotangent[micro_step].astype(jnp.float32)
        dout_low = dout.astype(jnp.bfloat16)
        grad_down = matmul(act_low.T, dout_low)
        grad_act = matmul(dout_low, down_w.T)
        (grad_upward,) = gelu_back(grad_act)
        up_low = grad_upward.astype(jnp.bfloat16)
        grad_upw = matmul(mid_low.T, up_low)
        grad_mid = matmul(up_low, up_w.T)
        dhid_norm, grad_gmlp, grad_bmlp = mid_back(grad_mid)
        dhidden = dout + dhid_norm
        dhid_low = dhidden.astype(jnp.bfloat16)
        grad_outw = matmul(att_low.T, dhid_low)
        grad_att = matmul(dhid_low, output_w.T).astype(jnp.bfloat16)
        grad_heads = grad_att.reshape(lat_rows, head_count, value_head)
        delta = jnp.sum(
            jnp.transpose(grad_heads.astype(jnp.float32), (1, 0, 2)) * attended, axis=-1
        )
        dquery_local, dscores, probs = query_part(
            queries, grad_heads, log_total, delta, keys, values, key_start, length, score_scale
        )
        dkeys = (
            (
                jnp.einsum("hlk,lhd->khd", dscores, queries, preferred_element_type=jnp.float32)
                * score_scale
            )
            .astype(jnp.bfloat16)
            .reshape(slot_count, -1)
        )
        dvalues = (
            jnp.einsum(
                "hlk,lhe->khe",
                probs.astype(jnp.bfloat16),
                grad_heads,
                preferred_element_type=jnp.float32,
            )
            .astype(jnp.bfloat16)
            .reshape(slot_count, -1)
        )

        def fold_add_block(carried, key_block, value_block, block_start):
            return (
                carried
                + query_part(
                    queries,
                    grad_heads,
                    log_total,
                    delta,
                    key_block,
                    value_block,
                    block_start,
                    length,
                    score_scale,
                )[0]
            )

        dquery = blocked(
            fold_add_block,
            jnp.zeros((lat_rows, head_count, head_size), jnp.float32),
            lax.all_gather(keys, "ctx", axis=0, tiled=True),
            lax.all_gather(values, "ctx", axis=0, tiled=True),
        )
        dquery_low = dquery.reshape(lat_rows, -1).astype(jnp.bfloat16)
        grad_qw = matmul(lat_low.T, dquery_low)
        dnorm_lat = matmul(dquery_low, query_w.T)
        dlat_norm, grad_glat, grad_blat = lat_back(dnorm_lat)
        grad_lat = dhidden + dlat_norm
        grad_kw = matmul(input_low.T, dkeys)
        grad_vw = matmul(input_low.T, dvalues)
        dnorm_in = matmul(dkeys, key_w.T) + matmul(dvalues, value_w.T)
        dfeatures, grad_gin, grad_bin = in_back(dnorm_in)
        byte_grads.append(dfeatures.astype(jnp.bfloat16))
        step_grads = [
            grad_lat,
            grad_glat,
            grad_blat,
            grad_gin,
            grad_bin,
            grad_qw,
            grad_kw,
            grad_vw,
            grad_outw,
            grad_gmlp,
            grad_bmlp,
            grad_upw,
            grad_down,
        ]
        if totals is None:
            totals = step_grads
        else:
            totals = [older + newer for older, newer in zip(totals, step_grads)]
    shares = (
        lax.psum_scatter(
            totals[0].astype(jnp.bfloat16), "wshard", scatter_dimension=0, tiled=True
        ).astype(jnp.float32),
        lax.psum_scatter(
            totals[1].astype(jnp.bfloat16), "wshard", scatter_dimension=0, tiled=True
        ).astype(jnp.float32),
        lax.psum_scatter(
            totals[2].astype(jnp.bfloat16), "wshard", scatter_dimension=0, tiled=True
        ).astype(jnp.float32),
        lax.psum_scatter(
            totals[3].astype(jnp.bfloat16), "wshard", scatter_dimension=0, tiled=True
        ).astype(jnp.float32),
        lax.psum_scatter(
            totals[4].astype(jnp.bfloat16), "wshard", scatter_dimension=0, tiled=True
        ).astype(jnp.float32),
        lax.psum_scatter(
            totals[5].astype(jnp.bfloat16), "wshard", scatter_dimension=0, tiled=True
        ).astype(jnp.float32),
        lax.psum_scatter(
            totals[6].astype(jnp.bfloat16), "wshard", scatter_dimension=0, tiled=True
        ).astype(jnp.float32),
        lax.psum_scatter(
            totals[7].astype(jnp.bfloat16), "wshard", scatter_dimension=0, tiled=True
        ).astype(jnp.float32),
        lax.psum_scatter(
            totals[8].astype(jnp.bfloat16), "wshard", scatter_dimension=0, tiled=True
        ).astype(jnp.float32),
        lax.psum_scatter(
            totals[9].astype(jnp.bfloat16), "wshard", scatter_dimension=0, tiled=True
        ).astype(jnp.float32),
        lax.psum_scatter(
            totals[10].astype(jnp.bfloat16), "wshard", scatter_dimension=0, tiled=True
        ).astype(jnp.float32),
        lax.psum_scatter(
            totals[11].astype(jnp.bfloat16), "wshard", scatter_dimension=0, tiled=True
        ).astype(jnp.float32),
        lax.psum_scatter(
            totals[12].astype(jnp.bfloat16), "wshard", scatter_dimension=0, tiled=True
        ).astype(jnp.float32),
    )
    summed = (
        lax.psum(shares[3].astype(jnp.bfloat16), "ctx").astype(jnp.float32),
        lax.psum(shares[4].astype(jnp.bfloat16), "ctx").astype(jnp.float32),
        lax.psum(shares[6].astype(jnp.bfloat16), "ctx").astype(jnp.float32),
        lax.psum(shares[7].astype(jnp.bfloat16), "ctx").astype(jnp.float32),
    )
    return (
        jnp.stack(latent_outs),
        jnp.stack(byte_grads),
        shares[0],
        shares[1],
        shares[2],
        summed[0],
        summed[1],
        shares[5],
        summed[2],
        summed[3],
        shares[8],
        shares[9],
        shares[10],
        shares[11],
        shares[12],
    )


def solution(mesh):
    placed = (
        P("wshard", "ctx", None),
        P("wshard"),
        P("wshard", None),
        P("wshard"),
        P("wshard"),
        P("wshard"),
        P("wshard"),
        P("wshard", None),
        P("wshard", None),
        P("wshard", None),
        P("wshard", None),
        P("wshard"),
        P("wshard"),
        P("wshard", None),
        P("wshard", None),
        P("wshard", None, None),
    )
    return jax.shard_map(
        shards,
        mesh=mesh,
        in_specs=placed,
        out_specs=(
            P("wshard", None, None),
            P("wshard", "ctx", None),
            P("wshard", None),
            P("wshard"),
            P("wshard"),
            P("wshard"),
            P("wshard"),
            P("wshard", None),
            P("wshard", None),
            P("wshard", None),
            P("wshard", None),
            P("wshard"),
            P("wshard"),
            P("wshard", None),
            P("wshard", None),
        ),
        check_vma=False,
    )
```

profile of v0, /device:TPU:0, one launch (start us, length us, event | category | flops | bytes accessed | tf_op | source)
XLA Modules:
  0.0 846.3 jit_solution(12040518271220998177)
XLA Ops:
  15.8 21.7 %all-reduce.15 = (bf16[768]{0:T(1024)(128)(2,1)S(1)}, bf16[768]{0:T(1024)(128)(2,1)S(1)}, bf16[1280]{0:T(1024)(128)(2,1)S(1)}, bf16[1280]{0:T(1024)(128)(2,1)S(1...) all-reduce(bf16[768]{0:T(1024)(128)(2,1)S(1)} %dynamic-update-slice, ...), channel_id=1, replica_groups=mesh['ctx'=8,'wshard'=4] {'wshard'}, use_global_device_ids=true, to_apply=%add.1 | all-reduce | flops 6656 | bytes 26624
  38.8 17.7 %all_gather.71 = bf16[768,256]{1,0:T(8,128)(2,1)S(1)} all-gather(bf16[192,256]{1,0:T(8,128)(2,1)S(1)} %copy-done.57), channel_id=1, replica_groups=mesh['ctx'=8,'wshard'=4] {'wshard'}, dimensions={0}, use_global_device_ids=true | all-gather | bytes 491520 | tf_op jit(solution)/shard_map/all_gather | solution.py:127
  71.0 17.1 %all_gather.68 = bf16[256,1280]{1,0:T(8,128)(2,1)S(1)} all-gather(bf16[64,1280]{1,0:T(8,128)(2,1)S(1)} %copy-done.53), channel_id=1, replica_groups=mesh['ctx'=8,'wshard'=4] {'wshard'}, dimensions={0}, use_global_device_ids=true | all-gather | bytes 819200 | tf_op jit(solution)/shard_map/all_gather | solution.py:121
  88.6 15.9 %all_gather.75 = bf16[1280,256]{1,0:T(8,128)(2,1)S(1)} all-gather(bf16[320,256]{1,0:T(8,128)(2,1)S(1)} %copy-done.54), channel_id=1, replica_groups=mesh['ctx'=8,'wshard'=4] {'wshard'}, dimensions={0}, use_global_device_ids=true | all-gather | bytes 819200 | tf_op jit(solution)/shard_map/all_gather | solution.py:126
  119.2 37.8 %all-gather.23.cloned.1.call-done = bf16[2048,1280]{1,0:T(8,128)(2,1)} async-done(((bf16[256,1280]{1,0:T(8,128)(2,1)}), bf16[2048,1280]{1,0:T(8,128)(2,1)}) %all-gather.23.cloned.1.call-update) | async-done | bytes 5242896 | tf_op jit(solution)/shard_map/all_gather | solution.py:184
  157.0 8.1 copy.70
  165.1 35.3 %all-gather.13.cloned.1.call-done = bf16[2048,1280]{1,0:T(8,128)(2,1)} async-done(((bf16[256,1280]{1,0:T(8,128)(2,1)}), bf16[2048,1280]{1,0:T(8,128)(2,1)}) %all-gather.13.cloned.1.call-update) | async-done | bytes 5242896 | tf_op jit(solution)/shard_map/all_gather | solution.py:184
  200.4 8.0 copy.68
  208.4 25.4 %while.53 = (s32[]{:T(128)}, f32[8,256]{1,0:T(8,128)S(1)}, f32[8,256]{1,0:T(8,128)S(1)}, f32[8,256,160]{1,2,0:T(8,128)}, s32[2]{0:T(128)S(1)}, /*index=5*/s32[]{...) while((s32[]{:T(128)}, f32[8,256]{1,0:T(8,128)S(1)}, ...), condition=%wide.region_15.16_spmd.clone, body=%wide.region_12.15_spmd.clone.sunk | while | flops 833894400 | bytes 47960292 | solution.py:88
  234.8 25.6 %while.52 = (s32[]{:T(128)}, f32[8,256]{1,0:T(8,128)S(1)}, f32[8,256]{1,0:T(8,128)S(1)}, f32[8,256,160]{1,2,0:T(8,128)}, s32[2]{0:T(128)S(1)}, /*index=5*/s32[]{...) while((s32[]{:T(128)}, f32[8,256]{1,0:T(8,128)S(1)}, ...), condition=%wide.region_7.8_spmd.clone, body=%wide.region_4.7_spmd.clone.sunk | while | flops 833894400 | bytes 47960292 | solution.py:88
  275.5 58.0 %all-gather.17.cloned.1.call-done = bf16[1280,1280]{1,0:T(8,128)(2,1)} async-done(((bf16[320,1280]{1,0:T(8,128)(2,1)}), bf16[1280,1280]{1,0:T(8,128)(2,1)}) %all-gather.17.cloned.1.call-update) | async-done | bytes 3276816 | tf_op jit(solution)/shard_map/all_gather | solution.py:132
  333.4 7.7 multiply_convert_fusion.18
  346.6 52.8 %all-gather.19.cloned.1.call-done = bf16[1280,1280]{1,0:T(8,128)(2,1)} async-done(((bf16[320,1280]{1,0:T(8,128)(2,1)}), bf16[1280,1280]{1,0:T(8,128)(2,1)}) %all-gather.19.cloned.1.call-update) | async-done | bytes 3276816 | tf_op jit(solution)/shard_map/all_gather | solution.py:133
  427.6 34.5 %while.55 = (s32[]{:T(128)}, f32[256,8,32]{0,2,1:T(8,128)S(1)}, bf16[2,1024,256]{1,2,0:T(8,128)(2,1)}, s32[2]{0:T(128)S(1)}, s32[]{:T(128)}, /*index=5*/bf16[256...) while((s32[]{:T(128)}, f32[256,8,32]{0,2,1:T(8,128)S(1)}, ...), condition=%wide.region_33.34_spmd.clone, body=%wide.region_32.33_spmd.clone.sunk | while | flops 952305664 | bytes 27543732 | solution.py:88
  438.3 6.7 fusion.338
  455.5 6.7 fusion.338
  482.6 30.5 %while.54 = (s32[]{:T(128)}, f32[256,8,32]{0,2,1:T(8,128)S(1)}, bf16[2,1024,256]{1,2,0:T(8,128)(2,1)S(1)}, s32[2]{0:T(128)S(1)}, s32[]{:T(128)}, /*index=5*/bf16...) while((s32[]{:T(128)}, f32[256,8,32]{0,2,1:T(8,128)S(1)}, ...), condition=%wide.region_29.30_spmd.clone, body=%wide.region_28.29_spmd.clone.sunk | while | flops 952305664 | bytes 27543732 | solution.py:88
  528.2 9.5 %reduce-scatter.14.cloned.1.call-done = bf16[192,1280]{1,0:T(8,128)(2,1)} async-done(((bf16[768,1280]{1,0:T(8,128)(2,1)}), bf16[192,1280]{1,0:T(8,128)(2,1)}) %reduce-scatter.14.cloned.1.call-update) | async-done | bytes 491536 | tf_op jit(solution)/shard_map/reduce_scatter | solution.py:311
  562.5 17.7 %all-reduce.14 = (bf16[1280]{0:T(1024)(128)(2,1)S(1)}, bf16[1280]{0:T(1024)(128)(2,1)S(1)}, bf16[768]{0:T(1024)(128)(2,1)S(1)}, bf16[768]{0:T(1024)(128)(2,1)S(1...) all-reduce(bf16[1280]{0:T(1024)(128)(2,1)S(1)} %add_convert_fusion., ...), channel_id=3, replica_groups=mesh['ctx'=8,'wshard'=4] {'wshard'}, use_global_device_ids=true, to_apply=%region_39.40.clone | all-reduce | flops 6656 | bytes 26624
  580.4 12.0 %all-reduce.12 = (bf16[192]{0:T(256)(128)(2,1)S(1)}, bf16[192]{0:T(256)(128)(2,1)S(1)}) all-reduce(bf16[192]{0:T(256)(128)(2,1)S(1)} %dynamic-slice.11, bf16[192]{0:T(256)(128)(2,1)S(1)} %dynamic-slice.13), channel_id=1, replica_groups=mesh['ctx'=8,'wshard'=4] {'ctx'}, use_global_device_ids=true, to_apply=%region_46.47 | all-reduce | flops 384 | bytes 1536 | tf_op jit(solution)/shard_map/psum | solution.py:331
  607.2 36.8 %all-reduce.18.cloned.1.call-done = (bf16[192,256]{1,0:T(8,128)(2,1)}, bf16[192,1280]{1,0:T(8,128)(2,1)}) async-done(((bf16[192,256]{1,0:T(8,128)(2,1)}, bf16[192,1280]{1,0:T(8,128)(2,1)}), (bf16[192,256]{1,0:T(8,128)(2,1)}, bf16[192,1280]{1,0:T(8,128)(2,1)})) %all-reduce.18.cloned.1.call-update) | async-done | bytes 589840 | tf_op jit(solution)/shard_map/psum | solution.py:333
  647.6 60.1 %reduce-scatter.18.cloned.1.call-done = bf16[320,1280]{1,0:T(8,128)(2,1)} async-done(((bf16[1280,1280]{1,0:T(8,128)(2,1)}), bf16[320,1280]{1,0:T(8,128)(2,1)}) %reduce-scatter.18.cloned.1.call-update) | async-done | bytes 819216 | tf_op jit(solution)/shard_map/reduce_scatter | solution.py:323
  710.1 62.2 %reduce-scatter.16.cloned.1.call-done = bf16[320,1280]{1,0:T(8,128)(2,1)} async-done(((bf16[1280,1280]{1,0:T(8,128)(2,1)}), bf16[320,1280]{1,0:T(8,128)(2,1)}) %reduce-scatter.16.cloned.1.call-update) | async-done | bytes 819216 | tf_op jit(solution)/shard_map/reduce_scatter | solution.py:314
  774.8 62.2 %reduce-scatter.20.cloned.1.call-done = bf16[320,1280]{1,0:T(8,128)(2,1)} async-done(((bf16[1280,1280]{1,0:T(8,128)(2,1)}), bf16[320,1280]{1,0:T(8,128)(2,1)}) %reduce-scatter.20.cloned.1.call-update) | async-done | bytes 819216 | tf_op jit(solution)/shard_map/reduce_scatter | solution.py:326
  (495 shorter events, 267.3 us)
Async XLA Ops:
  7.2 49.4 %copy-start.3 = (bf16[2,256,768]{2,1,0:T(8,128)(2,1)S(1)}, bf16[2,256,768]{2,1,0:T(8,128)(2,1)}, u32[]{:S(2)}) copy-start(bf16[2,256,768]{2,1,0:T(8,128)(2,1)} %param.24) | copy-start | bytes 2359300
  7.2 55.9 %all-gather.11.cloned.1.call-start = ((), (), s32[]{:S(2)}) async-start(), calls=%async_computation.8 | async-start | bytes 2457600 | tf_op jit(solution)/shard_map/all_gather | solution.py:128
  7.9 99.1 %all-gather.21.cloned.1.call-start = ((), (), s32[]{:S(2)}) async-start(), calls=%async_computation.13 | async-start | bytes 1179648 | tf_op jit(solution)/shard_map/all_gather | solution.py:183
  58.1 55.4 %all-gather.9.cloned.1.call-start = ((), (), s32[]{:S(2)}) async-start(), calls=%async_computation.7 | async-start | bytes 1179648 | tf_op jit(solution)/shard_map/all_gather | solution.py:183
  59.3 97.7 %all-gather.23.cloned.1.call-start = ((), (), s32[]{:S(2)}) async-start(), calls=%async_computation.14 | async-start | bytes 5898240 | tf_op jit(solution)/shard_map/all_gather | solution.py:184
  66.4 134.0 %all-gather.13.cloned.1.call-start = ((), (), s32[]{:S(2)}) async-start(), calls=%async_computation.9 | async-start | bytes 5898240 | tf_op jit(solution)/shard_map/all_gather | solution.py:184
  68.1 199.4 %all-gather.15.cloned.1.call-start = ((), (), s32[]{:S(2)}) async-start(), calls=%async_computation.10 | async-start | bytes 4096000 | tf_op jit(solution)/shard_map/all_gather | solution.py:129
  68.7 264.7 %all-gather.17.cloned.1.call-start = ((), (), s32[]{:S(2)}) async-start(), calls=%async_computation.11 | async-start | bytes 4096000 | tf_op jit(solution)/shard_map/all_gather | solution.py:132
  69.5 329.9 %all-gather.19.cloned.1.call-start = ((), (), s32[]{:S(2)}) async-start(), calls=%async_computation.12 | async-start | bytes 4096000 | tf_op jit(solution)/shard_map/all_gather | solution.py:133
  70.2 458.0 %reduce-scatter.12.cloned.1.call-start = ((), (), s32[]{:S(2)}) async-start(), calls=%async_computation.17 | async-start | bytes 491520 | tf_op jit(solution)/shard_map/reduce_scatter | solution.py:308
  270.9 138.7 %copy-start.1 = (f32[256,1280]{1,0:T(8,128)}, f32[256,1280]{1,0:T(8,128)S(1)}, u32[]{:S(2)}) copy-start(f32[256,1280]{1,0:T(8,128)S(1)} %get-tuple-element.630) | copy-start | bytes 3932164
  271.0 138.7 %copy-start.77 = (f32[256]{0:T(256)}, f32[256]{0:T(256)S(1)}, u32[]{:S(2)}) copy-start(f32[256]{0:T(256)S(1)} %broadcast_multiply_fusion.1) | copy-start | bytes 3076
  274.1 135.6 %copy-start.84 = (f32[256]{0:T(256)}, f32[256]{0:T(256)S(1)}, u32[]{:S(2)}) copy-start(f32[256]{0:T(256)S(1)} %broadcast_multiply_fusion) | copy-start | bytes 3076
  275.4 134.3 %copy-start.86 = (f32[256]{0:T(256)}, f32[256]{0:T(256)S(1)}, u32[]{:S(2)}) copy-start(f32[256]{0:T(256)S(1)} %fusion.163) | copy-start | bytes 3076
  275.4 134.3 %copy-start.99 = (f32[256]{0:T(256)}, f32[256]{0:T(256)S(1)}, u32[]{:S(2)}) copy-start(f32[256]{0:T(256)S(1)} %fusion.165) | copy-start | bytes 3076
  275.4 143.7 %copy-start.105 = (f32[8,256]{1,0:T(8,128)}, f32[8,256]{1,0:T(8,128)S(1)}, u32[]{:S(2)}) copy-start(f32[8,256]{1,0:T(8,128)S(1)} %log_add_fusion.1) | copy-start | bytes 24580
  427.6 36.5 %copy-start.67 = (f32[8,256]{1,0:T(8,128)S(1)}, f32[8,256]{1,0:T(8,128)}, u32[]{:S(2)}) copy-start(f32[8,256]{1,0:T(8,128)} %fusion.84) | copy-start | bytes 24580
  476.4 61.4 %reduce-scatter.14.cloned.1.call-start = ((), (), s32[]{:S(2)}) async-start(), calls=%async_computation.18 | async-start | bytes 2457600 | tf_op jit(solution)/shard_map/reduce_scatter | solution.py:311
  481.7 122.2 %reduce-scatter.8.cloned.1.call-start = ((), (), s32[]{:S(2)}) async-start(), calls=%async_computation.15 | async-start | bytes 819200 | tf_op jit(solution)/shard_map/reduce_scatter | solution.py:290
  520.9 84.6 %reduce-scatter.10.cloned.1.call-start = ((), (), s32[]{:S(2)}) async-start(), calls=%async_computation.16 | async-start | bytes 819200 | tf_op jit(solution)/shard_map/reduce_scatter | solution.py:305
  522.9 121.0 %all-reduce.18.cloned.1.call-start = ((), (), s32[]{:S(2)}) async-start(), calls=%async_computation.22 | async-start | bytes 1179648 | tf_op jit(solution)/shard_map/psum | solution.py:333
  537.8 169.9 %reduce-scatter.18.cloned.1.call-start = ((), (), s32[]{:S(2)}) async-start(), calls=%async_computation.20 | async-start | bytes 4096000 | tf_op jit(solution)/shard_map/reduce_scatter | solution.py:323
  543.6 228.7 %reduce-scatter.16.cloned.1.call-start = ((), (), s32[]{:S(2)}) async-start(), calls=%async_computation.19 | async-start | bytes 4096000 | tf_op jit(solution)/shard_map/reduce_scatter | solution.py:314
  549.7 287.2 %reduce-scatter.20.cloned.1.call-start = ((), (), s32[]{:S(2)}) async-start(), calls=%async_computation.21 | async-start | bytes 4096000 | tf_op jit(solution)/shard_map/reduce_scatter | solution.py:326
  (121 other events, 611.5 us)
Sparse Core Ops, SparseCore 0:
  9.6 53.4 all-gather.10
  65.5 22.4 all-gather.20
  89.9 23.5 all-gather.8
  115.8 41.1 all-gather.22
  159.3 41.1 all-gather.12
  201.8 65.6 all-gather.14
  269.1 64.2 all-gather.16
  335.0 64.2 all-gather.18
  476.5 19.2 reduce-scatter.11
  498.0 39.6 reduce-scatter.13
  540.7 21.3 reduce-scatter.7
  565.0 21.3 reduce-scatter.9
  589.9 54.0 all-reduce.17
  646.1 61.5 reduce-scatter.17
  709.9 62.4 reduce-scatter.15
  774.5 62.3 reduce-scatter.19
where the time goes:
time: 854 us; the launch traced here: 846 us
  waiting for transfers between devices  431 us (50%)
  matrix products  153 us (18%)
  blocking collectives  102 us (12%)
  local copies, waits for them, and re-layouts  79.7 us (9%)
  other arithmetic  54.5 us (6%)
  between operations  18.7 us (2%)
    dot_general x35, matrix products, matmul(): return jnp.dot(left, right, preferred_element_type=jnp.float32)  76.7 us
    all_gather x2, waiting for transfers between devices, shards(): lax.all_gather(values, 'ctx', axis=0, tiled=True)  73.1 us
    reduce_scatter x1, waiting for transfers between devices, shards(): lax.psum_scatter(totals[8].astype(jnp.bfloat16), 'wshard', scatter_dimens...  62.2 us
    reduce_scatter x1, waiting for transfers between devices, shards(): lax.psum_scatter(totals[12].astype(jnp.bfloat16), 'wshard', scatter_dimen...  62.2 us
    reduce_scatter x1, waiting for transfers between devices, shards(): lax.psum_scatter(totals[11].astype(jnp.bfloat16), 'wshard', scatter_dimen...  60.1 us
    all_gather x1, waiting for transfers between devices, shards(): lax.all_gather(w_up, 'wshard', axis=0, tiled=True)  58 us
    all_gather x1, waiting for transfers between devices, shards(): lax.all_gather(w_down, 'wshard', axis=0, tiled=True)  52.8 us
    unnamed x259, local copies, waits for them, and re-layouts  40.3 us
  transfers between devices with their start and end apart: 16, of which 12 were waited for; matrix products, arithmetic and copies ran while one was open for 23% of the time, Pallas kernels for 0%

commit v1 on v0

--- a/solution.py
+++ b/solution.py
@@ -330,7 +330,9 @@
     summed = (
         lax.psum(shares[3].astype(jnp.bfloat16), "ctx").astype(jnp.float32),
         lax.psum(shares[4].astype(jnp.bfloat16), "ctx").astype(jnp.float32),
-        lax.psum(shares[6].astype(jnp.bfloat16), "ctx").astype(jnp.float32),
+        jnp.sum(lax.all_gather(shares[6].astype(jnp.bfloat16), axis_name="ctx"), axis=0).astype(
+            jnp.float32
+        ),
         lax.psum(shares[7].astype(jnp.bfloat16), "ctx").astype(jnp.float32),
     )
     return (

time: 854 us -> 855 us (level)
  waiting for transfers between devices: 431 us -> 417 us
  blocking collectives: 102 us -> 112 us
    all_gather x0 -> x1, blocking collectives: none -> 10.6 us  [shards(): lax.all_gather(shares[6].astype(jnp.bfloat16), axis_name='ctx')]
    reduce_scatter x1, waiting for transfers between devices: 9.55 us -> 0.01 us  [shards(): lax.psum_scatter(totals[7].astype(jnp.bfloat16), 'wshard', scatter_dimens...]
    unnamed x259 -> x263, local copies, waits for them, and re-layouts: 40.3 us -> 39.4 us
  transfers between devices with their start and end apart: 16 -> 16, of which waited for: 12 -> 11; matrix products, arithmetic and copies ran while one was open for 23% -> 24% of each run, Pallas kernels for 0% -> 0%
where the time goes in v1:
time: 855 us; the launch traced here: 847 us
  waiting for transfers between devices  417 us (49%)
  matrix products  155 us (18%)
  blocking collectives  112 us (13%)
  local copies, waits for them, and re-layouts  80.7 us (9%)
  other arithmetic  55.8 us (7%)
  between operations  19 us (2%)
    dot_general x35, matrix products, matmul(): return jnp.dot(left, right, preferred_element_type=jnp.float32)  79 us
    all_gather x2, waiting for transfers between devices, shards(): lax.all_gather(values, 'ctx', axis=0, tiled=True)  73.1 us
    reduce_scatter x1, waiting for transfers between devices, shards(): lax.psum_scatter(totals[11].astype(jnp.bfloat16), 'wshard', scatter_dimen...  62.5 us
    reduce_scatter x1, waiting for transfers between devices, shards(): lax.psum_scatter(totals[12].astype(jnp.bfloat16), 'wshard', scatter_dimen...  62.2 us
    reduce_scatter x1, waiting for transfers between devices, shards(): lax.psum_scatter(totals[8].astype(jnp.bfloat16), 'wshard', scatter_dimens...  62.2 us
    all_gather x1, waiting for transfers between devices, shards(): lax.all_gather(w_up, 'wshard', axis=0, tiled=True)  58 us
    all_gather x1, waiting for transfers between devices, shards(): lax.all_gather(w_down, 'wshard', axis=0, tiled=True)  52.7 us
    unnamed x263, local copies, waits for them, and re-layouts  39.4 us
  transfers between devices with their start and end apart: 16, of which 11 were waited for; matrix products, arithmetic and copies ran while one was open for 24% of the time, Pallas kernels for 0%

profile of v1, /device:TPU:0, one launch (start us, length us, event | category | flops | bytes accessed | tf_op | source)
XLA Modules:
  0.0 846.8 jit_solution(8827915949448471814)
XLA Ops:
  15.8 21.7 %all-reduce.14 = (bf16[768]{0:T(1024)(128)(2,1)S(1)}, bf16[768]{0:T(1024)(128)(2,1)S(1)}, bf16[1280]{0:T(1024)(128)(2,1)S(1)}, bf16[1280]{0:T(1024)(128)(2,1)S(1...) all-reduce(bf16[768]{0:T(1024)(128)(2,1)S(1)} %dynamic-update-slice, ...), channel_id=1, replica_groups=mesh['ctx'=8,'wshard'=4] {'wshard'}, use_global_device_ids=true, to_apply=%add.1 | all-reduce | flops 6656 | bytes 26624
  38.9 17.7 %all_gather.77 = bf16[768,256]{1,0:T(8,128)(2,1)S(1)} all-gather(bf16[192,256]{1,0:T(8,128)(2,1)S(1)} %copy-done.59), channel_id=1, replica_groups=mesh['ctx'=8,'wshard'=4] {'wshard'}, dimensions={0}, use_global_device_ids=true | all-gather | bytes 491520 | tf_op jit(solution)/shard_map/all_gather | solution.py:127
  71.1 17.1 %all_gather.74 = bf16[256,1280]{1,0:T(8,128)(2,1)S(1)} all-gather(bf16[64,1280]{1,0:T(8,128)(2,1)S(1)} %copy-done.55), channel_id=1, replica_groups=mesh['ctx'=8,'wshard'=4] {'wshard'}, dimensions={0}, use_global_device_ids=true | all-gather | bytes 819200 | tf_op jit(solution)/shard_map/all_gather | solution.py:121
  88.7 15.9 %all_gather.81 = bf16[1280,256]{1,0:T(8,128)(2,1)S(1)} all-gather(bf16[320,256]{1,0:T(8,128)(2,1)S(1)} %copy-done.56), channel_id=1, replica_groups=mesh['ctx'=8,'wshard'=4] {'wshard'}, dimensions={0}, use_global_device_ids=true | all-gather | bytes 819200 | tf_op jit(solution)/shard_map/all_gather | solution.py:126
  119.2 37.8 %all-gather.24.cloned.1.call-done = bf16[2048,1280]{1,0:T(8,128)(2,1)} async-done(((bf16[256,1280]{1,0:T(8,128)(2,1)}), bf16[2048,1280]{1,0:T(8,128)(2,1)}) %all-gather.24.cloned.1.call-update) | async-done | bytes 5242896 | tf_op jit(solution)/shard_map/all_gather | solution.py:184
  157.0 8.2 copy.70
  165.1 35.3 %all-gather.14.cloned.1.call-done = bf16[2048,1280]{1,0:T(8,128)(2,1)} async-done(((bf16[256,1280]{1,0:T(8,128)(2,1)}), bf16[2048,1280]{1,0:T(8,128)(2,1)}) %all-gather.14.cloned.1.call-update) | async-done | bytes 5242896 | tf_op jit(solution)/shard_map/all_gather | solution.py:184
  200.4 7.9 copy.68
  208.3 25.5 %while.53 = (s32[]{:T(128)}, f32[8,256]{1,0:T(8,128)S(1)}, f32[8,256]{1,0:T(8,128)S(1)}, f32[8,256,160]{1,2,0:T(8,128)}, s32[2]{0:T(128)S(1)}, /*index=5*/s32[]{...) while((s32[]{:T(128)}, f32[8,256]{1,0:T(8,128)S(1)}, ...), condition=%wide.region_15.16_spmd.clone, body=%wide.region_12.15_spmd.clone.sunk | while | flops 833894400 | bytes 47960292 | solution.py:88
  234.8 25.5 %while.52 = (s32[]{:T(128)}, f32[8,256]{1,0:T(8,128)S(1)}, f32[8,256]{1,0:T(8,128)S(1)}, f32[8,256,160]{1,2,0:T(8,128)}, s32[2]{0:T(128)S(1)}, /*index=5*/s32[]{...) while((s32[]{:T(128)}, f32[8,256]{1,0:T(8,128)S(1)}, ...), condition=%wide.region_7.8_spmd.clone, body=%wide.region_4.7_spmd.clone.sunk | while | flops 833894400 | bytes 47960292 | solution.py:88
  275.4 58.0 %all-gather.18.cloned.1.call-done = bf16[1280,1280]{1,0:T(8,128)(2,1)} async-done(((bf16[320,1280]{1,0:T(8,128)(2,1)}), bf16[1280,1280]{1,0:T(8,128)(2,1)}) %all-gather.18.cloned.1.call-update) | async-done | bytes 3276816 | tf_op jit(solution)/shard_map/all_gather | solution.py:132
  333.4 7.8 multiply_convert_fusion.18
  346.6 52.7 %all-gather.20.cloned.1.call-done = bf16[1280,1280]{1,0:T(8,128)(2,1)} async-done(((bf16[320,1280]{1,0:T(8,128)(2,1)}), bf16[1280,1280]{1,0:T(8,128)(2,1)}) %all-gather.20.cloned.1.call-update) | async-done | bytes 3276816 | tf_op jit(solution)/shard_map/all_gather | solution.py:133
  429.3 34.8 %while.55 = (s32[]{:T(128)}, f32[256,8,32]{0,2,1:T(8,128)S(1)}, bf16[2,1024,256]{1,2,0:T(8,128)(2,1)}, s32[2]{0:T(128)S(1)}, s32[]{:T(128)}, /*index=5*/bf16[256...) while((s32[]{:T(128)}, f32[256,8,32]{0,2,1:T(8,128)S(1)}, ...), condition=%wide.region_33.34_spmd.clone, body=%wide.region_32.33_spmd.clone.sunk | while | flops 952305664 | bytes 27543732 | solution.py:88
  469.6 33.1 %while.54 = (s32[]{:T(128)}, f32[256,8,32]{0,2,1:T(8,128)S(1)}, bf16[2,1024,256]{1,2,0:T(8,128)(2,1)S(1)}, s32[2]{0:T(128)S(1)}, s32[]{:T(128)}, /*index=5*/bf16...) while((s32[]{:T(128)}, f32[256,8,32]{0,2,1:T(8,128)S(1)}, ...), condition=%wide.region_29.30_spmd.clone, body=%wide.region_28.29_spmd.clone.sunk | while | flops 952305664 | bytes 27543732 | solution.py:88
  479.6 6.8 fusion.331
  495.9 6.7 fusion.331
  558.3 16.1 %all-reduce.13 = (bf16[1280]{0:T(1024)(128)(2,1)S(1)}, bf16[1280]{0:T(1024)(128)(2,1)S(1)}, bf16[768]{0:T(1024)(128)(2,1)S(1)}, bf16[768]{0:T(1024)(128)(2,1)S(1...) all-reduce(bf16[1280]{0:T(1024)(128)(2,1)S(1)} %add_convert_fusion., ...), channel_id=4, replica_groups=mesh['ctx'=8,'wshard'=4] {'wshard'}, use_global_device_ids=true, to_apply=%region_39.40.clone | all-reduce | flops 6656 | bytes 26624
  574.6 12.6 %all-reduce.12 = (bf16[192]{0:T(256)(128)(2,1)S(1)}, bf16[192]{0:T(256)(128)(2,1)S(1)}) all-reduce(bf16[192]{0:T(256)(128)(2,1)S(1)} %dynamic-slice.11, bf16[192]{0:T(256)(128)(2,1)S(1)} %dynamic-slice.13), channel_id=1, replica_groups=mesh['ctx'=8,'wshard'=4] {'ctx'}, use_global_device_ids=true, to_apply=%region_46.47 | all-reduce | flops 384 | bytes 1536 | tf_op jit(solution)/shard_map/psum | solution.py:331
  598.7 10.6 %all-gather = bf16[1536,256]{1,0:T(8,128)(2,1)S(1)} all-gather(bf16[192,256]{1,0:T(8,128)(2,1)} %reduce-scatter.12.cloned.1.call-done), channel_id=2, replica_groups=mesh['ctx'=8,'wshard'=4] {'ctx'}, dimensions={0}, use_global_device_ids=true | all-gather | bytes 884736 | tf_op jit(solution)/shard_map/all_gather | solution.py:333
  613.4 30.1 %all-reduce.17.cloned.1.call-done = bf16[192,1280]{1,0:T(8,128)(2,1)} async-done(((bf16[192,1280]{1,0:T(8,128)(2,1)}), bf16[192,1280]{1,0:T(8,128)(2,1)}) %all-reduce.17.cloned.1.call-update) | async-done | bytes 491536 | tf_op jit(solution)/shard_map/psum | solution.py:336
  645.6 62.5 %reduce-scatter.18.cloned.1.call-done = bf16[320,1280]{1,0:T(8,128)(2,1)} async-done(((bf16[1280,1280]{1,0:T(8,128)(2,1)}), bf16[320,1280]{1,0:T(8,128)(2,1)}) %reduce-scatter.18.cloned.1.call-update) | async-done | bytes 819216 | tf_op jit(solution)/shard_map/reduce_scatter | solution.py:323
  710.5 62.2 %reduce-scatter.16.cloned.1.call-done = bf16[320,1280]{1,0:T(8,128)(2,1)} async-done(((bf16[1280,1280]{1,0:T(8,128)(2,1)}), bf16[320,1280]{1,0:T(8,128)(2,1)}) %reduce-scatter.16.cloned.1.call-update) | async-done | bytes 819216 | tf_op jit(solution)/shard_map/reduce_scatter | solution.py:314
  775.1 62.2 %reduce-scatter.20.cloned.1.call-done = bf16[320,1280]{1,0:T(8,128)(2,1)} async-done(((bf16[1280,1280]{1,0:T(8,128)(2,1)}), bf16[320,1280]{1,0:T(8,128)(2,1)}) %reduce-scatter.20.cloned.1.call-update) | async-done | bytes 819216 | tf_op jit(solution)/shard_map/reduce_scatter | solution.py:326
  (501 shorter events, 271.7 us)
Async XLA Ops:
  7.2 49.4 %copy-start.3 = (bf16[2,256,768]{2,1,0:T(8,128)(2,1)S(1)}, bf16[2,256,768]{2,1,0:T(8,128)(2,1)}, u32[]{:S(2)}) copy-start(bf16[2,256,768]{2,1,0:T(8,128)(2,1)} %param.24) | copy-start | bytes 2359300
  7.2 55.9 %all-gather.12.cloned.1.call-start = ((), (), s32[]{:S(2)}) async-start(), calls=%async_computation.8 | async-start | bytes 2457600 | tf_op jit(solution)/shard_map/all_gather | solution.py:128
  7.9 99.2 %all-gather.22.cloned.1.call-start = ((), (), s32[]{:S(2)}) async-start(), calls=%async_computation.13 | async-start | bytes 1179648 | tf_op jit(solution)/shard_map/all_gather | solution.py:183
  58.1 55.4 %all-gather.10.cloned.1.call-start = ((), (), s32[]{:S(2)}) async-start(), calls=%async_computation.7 | async-start | bytes 1179648 | tf_op jit(solution)/shard_map/all_gather | solution.py:183
  59.4 97.6 %all-gather.24.cloned.1.call-start = ((), (), s32[]{:S(2)}) async-start(), calls=%async_computation.14 | async-start | bytes 5898240 | tf_op jit(solution)/shard_map/all_gather | solution.py:184
  66.4 134.0 %all-gather.14.cloned.1.call-start = ((), (), s32[]{:S(2)}) async-start(), calls=%async_computation.9 | async-start | bytes 5898240 | tf_op jit(solution)/shard_map/all_gather | solution.py:184
  68.1 199.4 %all-gather.16.cloned.1.call-start = ((), (), s32[]{:S(2)}) async-start(), calls=%async_computation.10 | async-start | bytes 4096000 | tf_op jit(solution)/shard_map/all_gather | solution.py:129
  68.7 264.7 %all-gather.18.cloned.1.call-start = ((), (), s32[]{:S(2)}) async-start(), calls=%async_computation.11 | async-start | bytes 4096000 | tf_op jit(solution)/shard_map/all_gather | solution.py:132
  69.5 329.9 %all-gather.20.cloned.1.call-start = ((), (), s32[]{:S(2)}) async-start(), calls=%async_computation.12 | async-start | bytes 4096000 | tf_op jit(solution)/shard_map/all_gather | solution.py:133
  70.2 463.2 %reduce-scatter.14.cloned.1.call-start = ((), (), s32[]{:S(2)}) async-start(), calls=%async_computation.18 | async-start | bytes 2457600 | tf_op jit(solution)/shard_map/reduce_scatter | solution.py:311
  71.0 35.5 %copy-start.50 = (f32[1280]{0:T(1024)}, f32[1280]{0:T(1024)S(1)}, u32[]{:S(2)}) copy-start(f32[1280]{0:T(1024)S(1)} %convert_element_type.307) | copy-start | bytes 15364
  71.0 270.2 %copy-start.60 = (f32[1280]{0:T(1024)}, f32[1280]{0:T(1024)S(1)}, u32[]{:S(2)}) copy-start(f32[1280]{0:T(1024)S(1)} %convert_element_type.316) | copy-start | bytes 15364
  270.9 138.7 %copy-start.1 = (f32[256,1280]{1,0:T(8,128)}, f32[256,1280]{1,0:T(8,128)S(1)}, u32[]{:S(2)}) copy-start(f32[256,1280]{1,0:T(8,128)S(1)} %get-tuple-element.628) | copy-start | bytes 3932164
  271.0 138.7 %copy-start.81 = (f32[256]{0:T(256)}, f32[256]{0:T(256)S(1)}, u32[]{:S(2)}) copy-start(f32[256]{0:T(256)S(1)} %broadcast_multiply_fusion.1) | copy-start | bytes 3076
  274.1 135.6 %copy-start.89 = (f32[256]{0:T(256)}, f32[256]{0:T(256)S(1)}, u32[]{:S(2)}) copy-start(f32[256]{0:T(256)S(1)} %broadcast_multiply_fusion) | copy-start | bytes 3076
  275.4 134.3 %copy-start.91 = (f32[256]{0:T(256)}, f32[256]{0:T(256)S(1)}, u32[]{:S(2)}) copy-start(f32[256]{0:T(256)S(1)} %fusion.163) | copy-start | bytes 3076
  275.4 134.3 %copy-start.106 = (f32[256]{0:T(256)}, f32[256]{0:T(256)S(1)}, u32[]{:S(2)}) copy-start(f32[256]{0:T(256)S(1)} %fusion.165) | copy-start | bytes 3076
  468.7 130.0 %reduce-scatter.12.cloned.1.call-start = ((), (), s32[]{:S(2)}) async-start(), calls=%async_computation.17 | async-start | bytes 491520 | tf_op jit(solution)/shard_map/reduce_scatter | solution.py:308
  521.5 88.6 %reduce-scatter.8.cloned.1.call-start = ((), (), s32[]{:S(2)}) async-start(), calls=%async_computation.15 | async-start | bytes 819200 | tf_op jit(solution)/shard_map/reduce_scatter | solution.py:290
  525.1 86.6 %reduce-scatter.10.cloned.1.call-start = ((), (), s32[]{:S(2)}) async-start(), calls=%async_computation.16 | async-start | bytes 819200 | tf_op jit(solution)/shard_map/reduce_scatter | solution.py:305
  527.9 115.6 %all-reduce.17.cloned.1.call-start = ((), (), s32[]{:S(2)}) async-start(), calls=%async_computation.19 | async-start | bytes 983040 | tf_op jit(solution)/shard_map/psum | solution.py:336
  533.4 174.7 %reduce-scatter.18.cloned.1.call-start = ((), (), s32[]{:S(2)}) async-start(), calls=%async_computation.21 | async-start | bytes 4096000 | tf_op jit(solution)/shard_map/reduce_scatter | solution.py:323
  539.4 233.3 %reduce-scatter.16.cloned.1.call-start = ((), (), s32[]{:S(2)}) async-start(), calls=%async_computation.20 | async-start | bytes 4096000 | tf_op jit(solution)/shard_map/reduce_scatter | solution.py:314
  545.4 291.9 %reduce-scatter.20.cloned.1.call-start = ((), (), s32[]{:S(2)}) async-start(), calls=%async_computation.22 | async-start | bytes 4096000 | tf_op jit(solution)/shard_map/reduce_scatter | solution.py:326
  (123 other events, 668.0 us)
Sparse Core Ops, SparseCore 0:
  9.6 53.4 all-gather.11
  65.5 22.4 all-gather.21
  89.9 23.5 all-gather.9
  115.8 41.1 all-gather.23
  159.3 41.1 all-gather.13
  201.8 65.6 all-gather.15
  269.1 64.2 all-gather.17
  335.0 64.2 all-gather.19
  468.8 40.0 reduce-scatter.13
  521.6 18.9 reduce-scatter.11
  543.0 20.3 reduce-scatter.7
  566.2 21.0 reduce-scatter.9
  590.8 52.7 all-reduce.16
  645.7 62.3 reduce-scatter.17
  710.3 62.3 reduce-scatter.15
  774.9 62.3 reduce-scatter.19
